TPU v7x, 256 devices: a whole 4x4x8 slice. The times are simulated.
256 devices in a mesh: member: 32 (over x, y, core), grid: 8 (over z).
Axes of the slice: x: 4, y: 4, z: 8, core: 2. Of those that a mesh axis runs over, the one named last changes fastest.
Arguments:
- prior_ensemble: bfloat16 [512, 48, 32768], P('member', None, 'grid'), may hold values from -6 to 6
- measured_location: int32 [8, 32, 128], P('grid', 'member'), may hold values from 0 to 6143
- measured_tally: int32 [8, 32], P('grid', 'member'), may hold values from 32 to 128, as said below
- measured_reading: float32 [8, 32, 128], P('grid', 'member'), may hold values from -6 to 6
- measured_noise_sigma: float32 [8, 32, 128], P('grid', 'member'), may hold values from 0.5 to 20, as said below
Outputs:
- analysis: bfloat16 [512, 48, 32768], P('member', None, 'grid')
Inputs may be any that keep to these rules, and one draw needn't show every extreme that they name: `measured_location`: cell of the observation within its block of 48 rows and 128 columns. `measured_tally`: some block in every draw uses all 128 slots. `measured_noise_sigma`: positive error deviations.
All inputs are finite; a program needn't handle non-finite values.
Results may differ from a plain program's by a relative error of at most 0.0058.
Values may be sent and summed in bfloat16 or wider, within the bound.
A program may use at most 128 MiB of HBM per device.

v0:
```python
import jax
import jax.numpy as jnp
from jax import lax
from jax.sharding import PartitionSpec as P

HIGHEST_PRECISION = lax.Precision.HIGHEST


def whiten(hx_values, values, errors, obs_total):
    hx_float = hx_values.astype(jnp.float32)
    hx_mean = jnp.mean(hx_float, axis=0)
    usable = (jnp.arange(hx_values.shape[1], dtype=jnp.int32) < obs_total).astype(jnp.float32)
    scale_obs = usable / errors
    whitened = (hx_float - hx_mean) * scale_obs
    innovation = (values - hx_mean) * scale_obs
    return (whitened, innovation)


def transform_matrix(gram_total, drive_vector):
    members = gram_total.shape[0]
    identity = jnp.eye(members, dtype=jnp.float32)
    system = (members - 1.0) * identity + gram_total
    factor_low = jnp.linalg.cholesky(system)
    inverse = jax.scipy.linalg.solve_triangular(factor_low, identity, lower=True)
    inner = jnp.dot(inverse, drive_vector, precision=HIGHEST_PRECISION)
    mean_weight = jnp.dot(inverse.T, inner, precision=HIGHEST_PRECISION)
    spread = jnp.sqrt(members - 1.0) * inverse.T
    return (mean_weight[:, None] + spread).astype(jnp.bfloat16)


def local_sums(whitened, innovation):
    gram_local = lax.dot_general(
        whitened, whitened, (((1,), (1,)), ((), ())), precision=HIGHEST_PRECISION
    )
    drive_local = jnp.dot(whitened, innovation, precision=HIGHEST_PRECISION)
    return (gram_local, drive_local)


def reduce_gram(whitened, innovation):
    gram_local, drive_local = local_sums(whitened, innovation)
    gram_total, drive_vector = lax.psum((gram_local, drive_local), ("member", "grid"))
    return transform_matrix(gram_total, drive_vector)


def apply_block(state_block, transform):
    members, row_count, columns = state_block.shape
    flattened = state_block.reshape(members, row_count * columns)
    state_mean = jnp.mean(flattened.astype(jnp.float32), axis=0)
    anomalies = (flattened.astype(jnp.float32) - state_mean).astype(jnp.bfloat16)
    increment = lax.dot_general(
        transform, anomalies, (((0,), (0,)), ((), ())), preferred_element_type=jnp.float32
    )
    return (state_mean + increment).astype(jnp.bfloat16).reshape(members, row_count, columns)


def local(
    prior_ensemble, measured_location, measured_tally, measured_reading, measured_noise_sigma
):
    values = measured_reading[0, 0]
    errors = measured_noise_sigma[0, 0]
    obs_total = measured_tally[0, 0]
    shard_profiles = lax.all_to_all(
        prior_ensemble, "member", split_axis=2, concat_axis=0, tiled=True
    )
    members, row_count, columns = shard_profiles.shape
    hx_values = jnp.take(
        shard_profiles.reshape(members, row_count * columns), measured_location[0, 0], axis=1
    )
    whitened, innovation = whiten(hx_values, values, errors, obs_total)
    transform = reduce_gram(whitened, innovation)
    updated = apply_block(shard_profiles, transform)
    return lax.all_to_all(updated, "member", split_axis=0, concat_axis=2, tiled=True)


def solution(mesh):
    in_specs = (
        P("member", None, "grid"),
        P("grid", "member", None),
        P("grid", "member"),
        P("grid", "member", None),
        P("grid", "member", None),
    )
    out_specs = P("member", None, "grid")
    return jax.shard_map(local, mesh=mesh, in_specs=in_specs, out_specs=out_specs, check_vma=False)
```

profile of v0, /device:TPU:1, one launch (start us, length us, event | category | flops | bytes accessed | tf_op | source)
XLA Modules:
  0.0 763.0 jit_solution(7519993507879228197)
XLA Ops:
  6.5 19.4 %copy.19 = bf16[16,48,4096]{1,0,2:T(8,128)(2,1)} copy(bf16[16,48,4096]{2,1,0:T(8,128)(2,1)} %param.5) | data formatting | bytes 12582912 | tf_op args[0]
  25.9 31.8 %reshape.139 = bf16[32,2,49152]{2,1,0:T(2,128)(2,1)} reshape(bf16[4096,16,48]{2,1,0:T(8,128)(2,1)} %bitcast.111) | data formatting | bytes 12582912
  57.7 8.8 %all-to-all-start = ((bf16[32,2,49152]{2,1,0:T(2,128)(2,1)}), bf16[32,2,49152]{2,1,0:T(2,128)(2,1)}, u32[]{:S(2)}, u32[]{:S(2)}) async-start(bf16[32,2,49152]{2,1,0:T(2,128)(2,1)} %reshape.139), calls=%async_computation | async-start | bytes 12582912 | tf_op jit(solution)/shard_map/all_to_all | solution.py:62
  68.9 74.8 %all-to-all-done = bf16[32,2,49152]{2,1,0:T(2,128)(2,1)} async-done(((bf16[32,2,49152]{2,1,0:T(2,128)(2,1)}), bf16[32,2,49152]{2,1,0:T(2,128)(2,1)}, u32[]{:S(2)}, u32[]{:S(2)}) %all-to-all-start) | async-done | bytes 6291488 | tf_op jit(solution)/shard_map/all_to_all | solution.py:62
  143.7 27.6 %reshape.140 = bf16[4096,16,48]{2,1,0:T(8,128)(2,1)} reshape(bf16[32,2,49152]{2,1,0:T(2,128)(2,1)} %all-to-all-done) | data formatting | bytes 12582912
  171.3 18.8 %copy.20 = bf16[16,48,32,128]{3,1,0,2:T(8,128)(2,1)} copy(bf16[16,48,32,128]{1,0,3,2:T(8,128)(2,1)} %bitcast.110) | data formatting | bytes 12582912 | tf_op jit(solution)/shard_map/all_to_all | solution.py:62
  190.1 7.1 copy.44
  197.1 8.7 %copy.21 = bf16[512,6144]{0,1:T(8,128)(2,1)} copy(bf16[512,6144]{1,0:T(8,128)(2,1)} %bitcast.119) | data formatting | bytes 12582912 | tf_op jit(solution)/shard_map/reshape | solution.py:47
  205.8 4.5 gather_fusion
  210.5 2.2 fusion.20
  213.1 88.8 %psum.15 = f32[512]{0:T(512)S(1)} all-reduce(f32[512]{0:T(512)S(1)} %bitcast.121), channel_id=1, replica_groups=mesh['member'=32,'grid'=8] {'member','grid'}, use_global_device_ids=true, to_apply=%region_11.12 | all-reduce | flops 512 | bytes 4096 | tf_op jit(solution)/shard_map/psum | solution.py:41
  301.8 4.1 convert_reduce_fusion
  306.6 173.9 %all-reduce.3.cloned.1.call-done = f32[512,512]{0,1:T(8,128)} async-done(((f32[512,512]{0,1:T(8,128)}), f32[512,512]{0,1:T(8,128)}) %all-reduce.3.cloned.1.call-update) | async-done | bytes 1048592 | tf_op jit(solution)/shard_map/psum | solution.py:41
  483.6 11.7 %cholesky.107 = f32[128,128]{1,0:T(8,128)S(1)} custom-call(f32[128,128]{1,0:T(8,128)S(1)} %cholesky.269), custom_call_target="Cholesky" | custom-call | tf_op jit(solution)/shard_map/jit(cholesky)/cholesky | solution.py:23
  495.4 9.8 %custom-call.31 = f32[1,128,128]{1,2,0:T(8,128)S(1)} custom-call(f32[1,128,128]{2,1,0:T(8,128)S(1)} %get-tuple-element.36), custom_call_target="InvertDiagBlocksLowerTriangular" | custom-call | tf_op jit(solution)/shard_map/jit(cholesky)/cholesky | solution.py:23
  505.9 11.9 %cholesky.221 = f32[128,128]{1,0:T(8,128)S(1)} custom-call(f32[128,128]{1,0:T(8,128)S(1)} %cholesky.273), custom_call_target="Cholesky" | custom-call | tf_op jit(solution)/shard_map/jit(cholesky)/cholesky | solution.py:23
  518.1 9.8 %custom-call.32 = f32[1,128,128]{1,2,0:T(8,128)S(1)} custom-call(f32[1,128,128]{2,1,0:T(8,128)S(1)} %get-tuple-element.34), custom_call_target="InvertDiagBlocksLowerTriangular" | custom-call | tf_op jit(solution)/shard_map/jit(cholesky)/cholesky | solution.py:23
  530.7 13.2 %cholesky.242 = f32[128,128]{1,0:T(8,128)} custom-call(f32[128,128]{1,0:T(8,128)} %cholesky.278), custom_call_target="Cholesky" | custom-call | tf_op jit(solution)/shard_map/jit(cholesky)/cholesky | solution.py:23
  547.8 11.3 %custom-call.33 = f32[1,128,128]{1,2,0:T(8,128)} custom-call(f32[1,128,128]{2,1,0:T(8,128)} %get-tuple-element.32), custom_call_target="InvertDiagBlocksLowerTriangular" | custom-call | tf_op jit(solution)/shard_map/jit(cholesky)/cholesky | solution.py:23
  561.5 12.1 %cholesky.259 = f32[128,128]{1,0:T(8,128)S(1)} custom-call(f32[128,128]{1,0:T(8,128)S(1)} %convolution_subtract_fusion.5), custom_call_target="Cholesky" | custom-call | tf_op jit(solution)/shard_map/jit(cholesky)/cholesky | solution.py:23
  582.0 14.5 %while.1 = (s32[]{:T(128)}, f32[512,512]{0,1:T(8,128)}, s32[4,2]{0,1:T(2,128)S(1)}, f32[4,128,128]{2,1,0:T(8,128)}, s32[]{:T(128)}) while((s32[]{:T(128)}, f32[512,512]{0,1:T(8,128)}, s32[4,2]{0,1:T(2,128)S(1)}, f32[4,128,128]{2,1,0:T(8,128)}, s32[]{:T(128)}) %tuple.25), condition=%wide.while_cond, body=%wide.while_body.sunk | while | flops 2 | bytes 393829 | solution.py:24
  582.7 2.2 dynamic-slice.7
  586.3 2.2 dynamic-slice.7
  590.0 2.2 dynamic-slice.7
  596.5 40.1 %custom-call.34 = f32[4,128,128]{1,2,0:T(8,128)S(1)} custom-call(f32[4,128,128]{2,1,0:T(8,128)} %get-tuple-element.12), custom_call_target="InvertDiagBlocksLowerTriangular" | custom-call | tf_op jit(solution)/shard_map/jit(_solve_triangular)/triangular_solve | solution.py:24
  639.0 2.2 convolution_subtract_fusion
  641.7 2.5 convolution_subtract_fusion.2
  646.3 6.7 fusion.1
  653.0 4.7 copy.38
  657.7 81.4 %all_to_all.33 = bf16[512,48,128]{2,1,0:T(8,128)(2,1)S(1)} all-to-all(bf16[512,48,128]{2,1,0:T(8,128)(2,1)S(1)} %bitcast.116), channel_id=1, replica_groups=mesh['member'=32,'grid'=8] {'member'}, dimensions={0} | all-to-all | bytes 12582912 | tf_op jit(solution)/shard_map/all_to_all | solution.py:72
  739.0 6.7 copy.45
  745.7 10.3 %all_to_all.30 = bf16[16,48,4096]{2,1,0:T(8,128)(2,1)} reshape(bf16[16,48,32,128]{3,2,1,0:T(8,128)(2,1)} %bitcast.118) | data formatting | bytes 12582912 | tf_op jit(solution)/shard_map/all_to_all | solution.py:72
  (84 shorter events, 34.6 us)
Async XLA Ops:
  57.6 10.1 %copy-start.3 = (s32[1,1,128]{2,1,0:T(1,128)S(1)}, s32[1,1,128]{2,1,0:T(1,128)}, u32[]{:S(2)}) copy-start(s32[1,1,128]{2,1,0:T(1,128)} %param.6) | copy-start | bytes 1540
  57.7 86.1 %all-to-all-start = ((bf16[32,2,49152]{2,1,0:T(2,128)(2,1)}), bf16[32,2,49152]{2,1,0:T(2,128)(2,1)}, u32[]{:S(2)}, u32[]{:S(2)}) async-start(bf16[32,2,49152]{2,1,0:T(2,128)(2,1)} %reshape.139), calls=%async_computation | async-start | bytes 12582912 | tf_op jit(solution)/shard_map/all_to_all | solution.py:62
  66.4 414.0 %all-reduce.3.cloned.1.call-start = ((), (), s32[]{:S(2)}) async-start(), calls=%async_computation.2 | async-start | bytes 2097152 | tf_op jit(solution)/shard_map/psum | solution.py:41
  197.1 13.3 %copy-start.2 = (f32[1,1,128]{2,1,0:T(1,128)S(1)}, f32[1,1,128]{2,1,0:T(1,128)}, u32[]{:S(2)}) copy-start(f32[1,1,128]{2,1,0:T(1,128)} %param.9) | copy-start | bytes 1540
  197.1 15.6 %copy-start.4 = (f32[1,1,128]{2,1,0:T(1,128)S(1)}, f32[1,1,128]{2,1,0:T(1,128)}, u32[]{:S(2)}) copy-start(f32[1,1,128]{2,1,0:T(1,128)} %param.8) | copy-start | bytes 1540
  483.6 44.5 %copy-start = (f32[512,512]{1,0:T(8,128)}, f32[512,512]{1,0:T(8,128)S(1)}, u32[]{:S(2)}) copy-start(f32[512,512]{1,0:T(8,128)S(1)} %fusion.6) | copy-start | bytes 3145732
  528.5 117.8 %slice-start = ((s8[6291456]{0:T(1024)(128)(4,1)}), s8[2097152]{0:T(1024)(128)(4,1)S(1)}, s32[]{:S(2)}) async-start(s8[6291456]{0:T(1024)(128)(4,1)} %bitcast.113), calls=%async_computation.3 | async-start | bytes 4194304
  580.2 66.1 %copy-start.1 = (f32[6144]{0:T(1024)S(1)}, f32[6144]{0:T(1024)}, u32[]{:S(2)}) copy-start(f32[6144]{0:T(1024)} %multiply_bitcast_fusion) | copy-start | bytes 73732
  638.6 7.7 %slice-start.1 = ((s8[6291456]{0:T(1024)(128)(4,1)}), s8[4194304]{0:T(1024)(128)(4,1)S(1)}, s32[]{:S(2)}) async-start(s8[6291456]{0:T(1024)(128)(4,1)} %bitcast.113), calls=%async_computation.4 | async-start | bytes 8388608
Sparse Core Ops, SparseCore 0:
  212.8 267.5 all-reduce.2
where the time goes:
time: 773 us; the launch traced here: 763 us
  waiting for transfers between devices  249 us (32%)
  blocking collectives  170 us (22%)
  local copies, waits for them, and re-layouts  158 us (20%)
  other arithmetic  136 us (18%)
  matrix products  23.9 us (3%)
  between operations  17.1 us (2%)
  starting transfers between devices  8.8 us (1%)
    psum x1, waiting for transfers between devices, reduce_gram(): lax.psum((gram_local, drive_local), ('member', 'grid'))  174 us
    unnamed x19, local copies, waits for them, and re-layouts  90.5 us
    psum x1, blocking collectives, reduce_gram(): lax.psum((gram_local, drive_local), ('member', 'grid'))  88.8 us
    another operation x15, other arithmetic, transform_matrix(): factor_low = jnp.linalg.cholesky(system)  85.3 us
    all_to_all x1, blocking collectives, local(): lax.all_to_all(updated, 'member', split_axis=0, concat_axis=2, tiled=True)  81.4 us
    all_to_all x1, waiting for transfers between devices, local(): lax.all_to_all(prior_ensemble, 'member', split_axis=2, concat_axis=0, til...  74.8 us
    another operation x3, other arithmetic, transform_matrix(): jax.scipy.linalg.solve_triangular(factor_low, identity, lower=True)  41.8 us
    all_to_all x1, local copies, waits for them, and re-layouts, local(): lax.all_to_all(prior_ensemble, 'member', split_axis=2, concat_axis=0, til...  18.8 us
  transfers between devices with their start and end apart: 2, of which 2 were waited for; matrix products, arithmetic and copies ran while one was open for 1% of the time, Pallas kernels for 0%

commit v1 on v0

--- a/solution.py
+++ b/solution.py
@@ -37,8 +37,16 @@
 
 
 def reduce_gram(whitened, innovation):
+
+    def obtain_the_clusters(local_array):
+        axis_tag = "member"
+        bus_axis = "grid"
+        for m in (bus_axis, axis_tag):
+            local_array = lax.psum(local_array, m)
+        return local_array
+
     gram_local, drive_local = local_sums(whitened, innovation)
-    gram_total, drive_vector = lax.psum((gram_local, drive_local), ("member", "grid"))
+    gram_total, drive_vector = obtain_the_clusters((gram_local, drive_local))
     return transform_matrix(gram_total, drive_vector)
 
 

time: 773 us -> 705 us (0.912)
  waiting for transfers between devices: 249 us -> 183 us
    psum x1 -> x2, waiting for transfers between devices: 174 us -> 106 us  [obtain_the_clusters(): local_array = lax.psum(local_array, m)]
    psum x1 -> x2, blocking collectives: 88.8 us -> 89.8 us  [obtain_the_clusters(): local_array = lax.psum(local_array, m)]
  transfers between devices with their start and end apart: 2 -> 3, of which waited for: 2 -> 2; matrix products, arithmetic and copies ran while one was open for 1% -> 1% of each run, Pallas kernels for 0% -> 0%
where the time goes in v1:
time: 705 us; the launch traced here: 696 us
  waiting for transfers between devices  183 us (26%)
  blocking collectives  169 us (24%)
  local copies, waits for them, and re-layouts  158 us (22%)
  other arithmetic  136 us (19%)
  matrix products  23.8 us (3%)
  between operations  17.1 us (2%)
  starting transfers between devices  8.84 us (1%)
    psum x2, waiting for transfers between devices, obtain_the_clusters(): local_array = lax.psum(local_array, m)  106 us
    unnamed x19, local copies, waits for them, and re-layouts  90.5 us
    psum x2, blocking collectives, obtain_the_clusters(): local_array = lax.psum(local_array, m)  89.8 us
    another operation x15, other arithmetic, transform_matrix(): factor_low = jnp.linalg.cholesky(system)  85.2 us
    all_to_all x1, blocking collectives, local(): lax.all_to_all(updated, 'member', split_axis=0, concat_axis=2, tiled=True)  79 us
    all_to_all x1, waiting for transfers between devices, local(): lax.all_to_all(prior_ensemble, 'member', split_axis=2, concat_axis=0, til...  76.5 us
    another operation x3, other arithmetic, transform_matrix(): jax.scipy.linalg.solve_triangular(factor_low, identity, lower=True)  41.9 us
    all_to_all x1, local copies, waits for them, and re-layouts, local(): lax.all_to_all(prior_ensemble, 'member', split_axis=2, concat_axis=0, til...  18.8 us
  transfers between devices with their start and end apart: 3, of which 2 were waited for; matrix products, arithmetic and copies ran while one was open for 1% of the time, Pallas kernels for 0%

profile of v1, /device:TPU:1, one launch (start us, length us, event | category | flops | bytes accessed | tf_op | source)
XLA Modules:
  0.0 695.5 jit_solution(6034240774330629529)
XLA Ops:
  6.5 19.4 %copy.19 = bf16[16,48,4096]{1,0,2:T(8,128)(2,1)} copy(bf16[16,48,4096]{2,1,0:T(8,128)(2,1)} %param.5) | data formatting | bytes 12582912 | tf_op args[0]
  25.9 31.8 %reshape.139 = bf16[32,2,49152]{2,1,0:T(2,128)(2,1)} reshape(bf16[4096,16,48]{2,1,0:T(8,128)(2,1)} %bitcast.111) | data formatting | bytes 12582912
  57.7 8.8 %all-to-all-start = ((bf16[32,2,49152]{2,1,0:T(2,128)(2,1)}), bf16[32,2,49152]{2,1,0:T(2,128)(2,1)}, u32[]{:S(2)}, u32[]{:S(2)}) async-start(bf16[32,2,49152]{2,1,0:T(2,128)(2,1)} %reshape.139), calls=%async_computation | async-start | bytes 12582912 | tf_op jit(solution)/shard_map/all_to_all | solution.py:70
  67.2 76.5 %all-to-all-done = bf16[32,2,49152]{2,1,0:T(2,128)(2,1)} async-done(((bf16[32,2,49152]{2,1,0:T(2,128)(2,1)}), bf16[32,2,49152]{2,1,0:T(2,128)(2,1)}, u32[]{:S(2)}, u32[]{:S(2)}) %all-to-all-start) | async-done | bytes 6291488 | tf_op jit(solution)/shard_map/all_to_all | solution.py:70
  143.7 27.6 %reshape.140 = bf16[4096,16,48]{2,1,0:T(8,128)(2,1)} reshape(bf16[32,2,49152]{2,1,0:T(2,128)(2,1)} %all-to-all-done) | data formatting | bytes 12582912
  171.3 18.8 %copy.20 = bf16[16,48,32,128]{3,1,0,2:T(8,128)(2,1)} copy(bf16[16,48,32,128]{1,0,3,2:T(8,128)(2,1)} %bitcast.110) | data formatting | bytes 12582912 | tf_op jit(solution)/shard_map/all_to_all | solution.py:70
  190.1 7.1 %copy.44 = bf16[64,8,48,128]{3,1,2,0:T(8,128)(2,1)} copy(bf16[64,8,48,128]{3,2,1,0:T(8,128)(2,1)} %bitcast.112) | data formatting | bytes 12582912
  197.1 8.7 %copy.21 = bf16[512,6144]{0,1:T(8,128)(2,1)} copy(bf16[512,6144]{1,0:T(8,128)(2,1)} %bitcast.119) | data formatting | bytes 12582912 | tf_op jit(solution)/shard_map/reshape | solution.py:55
  205.8 4.5 gather_fusion
  214.8 16.2 %psum.30 = f32[512]{0:T(512)S(1)} all-reduce(f32[512]{0:T(512)S(1)} %bitcast.121), channel_id=1, replica_groups=mesh['member'=32,'grid'=8] {'grid'}, use_global_device_ids=true, to_apply=%region_12.13 | all-reduce | flops 512 | bytes 4096 | tf_op jit(solution)/shard_map/psum | solution.py:45
  231.1 73.6 %psum.31 = f32[512]{0:T(512)S(1)} all-reduce(f32[512]{0:T(512)S(1)} %psum.30), channel_id=1, replica_groups=mesh['member'=32,'grid'=8] {'member'}, use_global_device_ids=true, to_apply=%region_13.14 | all-reduce | flops 512 | bytes 4096 | tf_op jit(solution)/shard_map/psum | solution.py:45
  304.7 4.1 convert_reduce_fusion
  309.4 106.3 %all-reduce.6.cloned.1.call-done = f32[512,512]{0,1:T(8,128)} async-done(((f32[512,512]{0,1:T(8,128)}), f32[512,512]{0,1:T(8,128)}) %all-reduce.6.cloned.1.call-update) | async-done | bytes 1048592 | tf_op jit(solution)/shard_map/psum | solution.py:45
  418.9 11.7 %cholesky.107 = f32[128,128]{1,0:T(8,128)S(1)} custom-call(f32[128,128]{1,0:T(8,128)S(1)} %cholesky.269), custom_call_target="Cholesky" | custom-call | tf_op jit(solution)/shard_map/jit(cholesky)/cholesky | solution.py:23
  430.6 9.8 %custom-call.31 = f32[1,128,128]{1,2,0:T(8,128)S(1)} custom-call(f32[1,128,128]{2,1,0:T(8,128)S(1)} %get-tuple-element.36), custom_call_target="InvertDiagBlocksLowerTriangular" | custom-call | tf_op jit(solution)/shard_map/jit(cholesky)/cholesky | solution.py:23
  441.1 11.9 %cholesky.221 = f32[128,128]{1,0:T(8,128)S(1)} custom-call(f32[128,128]{1,0:T(8,128)S(1)} %cholesky.273), custom_call_target="Cholesky" | custom-call | tf_op jit(solution)/shard_map/jit(cholesky)/cholesky | solution.py:23
  453.4 9.8 %custom-call.32 = f32[1,128,128]{1,2,0:T(8,128)S(1)} custom-call(f32[1,128,128]{2,1,0:T(8,128)S(1)} %get-tuple-element.34), custom_call_target="InvertDiagBlocksLowerTriangular" | custom-call | tf_op jit(solution)/shard_map/jit(cholesky)/cholesky | solution.py:23
  466.0 13.2 %cholesky.242 = f32[128,128]{1,0:T(8,128)} custom-call(f32[128,128]{1,0:T(8,128)} %cholesky.278), custom_call_target="Cholesky" | custom-call | tf_op jit(solution)/shard_map/jit(cholesky)/cholesky | solution.py:23
  483.0 11.3 %custom-call.33 = f32[1,128,128]{1,2,0:T(8,128)} custom-call(f32[1,128,128]{2,1,0:T(8,128)} %get-tuple-element.32), custom_call_target="InvertDiagBlocksLowerTriangular" | custom-call | tf_op jit(solution)/shard_map/jit(cholesky)/cholesky | solution.py:23
  496.8 12.1 %cholesky.259 = f32[128,128]{1,0:T(8,128)S(1)} custom-call(f32[128,128]{1,0:T(8,128)S(1)} %convolution_subtract_fusion.5), custom_call_target="Cholesky" | custom-call | tf_op jit(solution)/shard_map/jit(cholesky)/cholesky | solution.py:23
  517.2 14.2 %while.1 = (s32[]{:T(128)}, f32[512,512]{0,1:T(8,128)}, s32[4,2]{0,1:T(2,128)S(1)}, f32[4,128,128]{2,1,0:T(8,128)}, s32[]{:T(128)}) while((s32[]{:T(128)}, f32[512,512]{0,1:T(8,128)}, s32[4,2]{0,1:T(2,128)S(1)}, f32[4,128,128]{2,1,0:T(8,128)}, s32[]{:T(128)}) %tuple.25), condition=%wide.while_cond, body=%wide.while_body.sunk | while | flops 2 | bytes 393829 | solution.py:24
  517.8 2.2 dynamic-slice.7
  521.4 2.2 dynamic-slice.7
  525.0 2.2 dynamic-slice.7
  531.4 40.1 %custom-call.34 = f32[4,128,128]{1,2,0:T(8,128)S(1)} custom-call(f32[4,128,128]{2,1,0:T(8,128)} %get-tuple-element.12), custom_call_target="InvertDiagBlocksLowerTriangular" | custom-call | tf_op jit(solution)/shard_map/jit(_solve_triangular)/triangular_solve | solution.py:24
  573.9 2.2 convolution_subtract_fusion
  576.6 2.5 convolution_subtract_fusion.2
  581.2 6.7 fusion.1
  587.9 4.7 copy.38
  592.6 79.0 %all_to_all.33 = bf16[512,48,128]{2,1,0:T(8,128)(2,1)S(1)} all-to-all(bf16[512,48,128]{2,1,0:T(8,128)(2,1)S(1)} %bitcast.116), channel_id=1, replica_groups=mesh['member'=32,'grid'=8] {'member'}, dimensions={0} | all-to-all | bytes 12582912 | tf_op jit(solution)/shard_map/all_to_all | solution.py:80
  671.5 6.7 copy.45
  678.2 10.3 %all_to_all.30 = bf16[16,48,4096]{2,1,0:T(8,128)(2,1)} reshape(bf16[16,48,32,128]{3,2,1,0:T(8,128)(2,1)} %bitcast.118) | data formatting | bytes 12582912 | tf_op jit(solution)/shard_map/all_to_all | solution.py:80
  (88 shorter events, 36.6 us)
Async XLA Ops:
  57.6 9.5 %copy-start.3 = (s32[1,1,128]{2,1,0:T(1,128)S(1)}, s32[1,1,128]{2,1,0:T(1,128)}, u32[]{:S(2)}) copy-start(s32[1,1,128]{2,1,0:T(1,128)} %param.6) | copy-start | bytes 1540
  57.7 86.1 %all-to-all-start = ((bf16[32,2,49152]{2,1,0:T(2,128)(2,1)}), bf16[32,2,49152]{2,1,0:T(2,128)(2,1)}, u32[]{:S(2)}, u32[]{:S(2)}) async-start(bf16[32,2,49152]{2,1,0:T(2,128)(2,1)} %reshape.139), calls=%async_computation | async-start | bytes 12582912 | tf_op jit(solution)/shard_map/all_to_all | solution.py:70
  66.4 238.3 %all-reduce.4.cloned.1.call-start = ((), (), s32[]{:S(2)}) async-start(), calls=%async_computation.2 | async-start | bytes 2097152 | tf_op jit(solution)/shard_map/psum | solution.py:45
  197.1 13.3 %copy-start.2 = (f32[1,1,128]{2,1,0:T(1,128)S(1)}, f32[1,1,128]{2,1,0:T(1,128)}, u32[]{:S(2)}) copy-start(f32[1,1,128]{2,1,0:T(1,128)} %param.9) | copy-start | bytes 1540
  197.1 17.4 %copy-start.4 = (f32[1,1,128]{2,1,0:T(1,128)S(1)}, f32[1,1,128]{2,1,0:T(1,128)}, u32[]{:S(2)}) copy-start(f32[1,1,128]{2,1,0:T(1,128)} %param.8) | copy-start | bytes 1540
  212.7 203.1 %all-reduce.6.cloned.1.call-start = ((), (), s32[]{:S(2)}) async-start(), calls=%async_computation.3 | async-start | bytes 2097152 | tf_op jit(solution)/shard_map/psum | solution.py:45
  418.9 44.5 %copy-start = (f32[512,512]{1,0:T(8,128)}, f32[512,512]{1,0:T(8,128)S(1)}, u32[]{:S(2)}) copy-start(f32[512,512]{1,0:T(8,128)S(1)} %fusion.6) | copy-start | bytes 3145732
  463.7 117.5 %slice-start = ((s8[6291456]{0:T(1024)(128)(4,1)}), s8[2097152]{0:T(1024)(128)(4,1)S(1)}, s32[]{:S(2)}) async-start(s8[6291456]{0:T(1024)(128)(4,1)} %bitcast.113), calls=%async_computation.4 | async-start | bytes 4194304
  515.3 65.8 %copy-start.1 = (f32[6144]{0:T(1024)S(1)}, f32[6144]{0:T(1024)}, u32[]{:S(2)}) copy-start(f32[6144]{0:T(1024)} %multiply_bitcast_fusion) | copy-start | bytes 73732
  573.5 7.7 %slice-start.1 = ((s8[6291456]{0:T(1024)(128)(4,1)}), s8[4194304]{0:T(1024)(128)(4,1)S(1)}, s32[]{:S(2)}) async-start(s8[6291456]{0:T(1024)(128)(4,1)} %bitcast.113), calls=%async_computation.5 | async-start | bytes 8388608
Sparse Core Ops, SparseCore 0:
  212.8 81.4 all-reduce.3
  304.8 110.8 all-reduce.5
